TPU v7x, 128 devices: a whole 4x4x4 slice. The times are simulated.
128 devices in a mesh: dp: 4 (over x), tensor: 32 (over y, z, core).
Axes of the slice: x: 4, y: 4, z: 4, core: 2. Of those that a mesh axis runs over, the one named last changes fastest.
Arguments:
- tokens: bfloat16 [16384, 2048], P(('dp', 'tensor')), may hold values from -6 to 6
- norm_gain: bfloat16 [2048], replicated, may hold values from 0.099609375 to 1.8984375
- routes: int32 [16384, 6], P(('dp', 'tensor')), may hold values from 0 to 31, all different within a row; in each aligned block of 128 rows (0 to 127, 128 to 255, ...) at most 32 rows name the same one
- route_gates: bfloat16 [16384, 6], P(('dp', 'tensor')), may hold values from 0.19921875 to 1
- lengths: int32 [24], replicated, may hold values from 1 to 1920, 16384 in all
- request_adapter: int32 [24], replicated, may hold values from 0 to 31
- adapter_slot: int32 [32], replicated, may hold values from 0 to 31, each once
- expert_gate: bfloat16 [32, 2048, 1408], P('tensor'), may hold values from -0.125 to 0.125
- expert_up: bfloat16 [32, 2048, 1408], P('tensor'), may hold values from -0.125 to 0.125
- expert_down: bfloat16 [32, 1408, 2048], P('tensor'), may hold values from -0.15625 to 0.15625
- shared_gate: bfloat16 [2048, 1408], P(None, 'dp'), may hold values from -0.125 to 0.125
- shared_up_weight: bfloat16 [2048, 1408], P(None, 'dp'), may hold values from -0.125 to 0.125
- shared_down: bfloat16 [1408, 2048], P('dp'), may hold values from -0.15625 to 0.15625
- adapter_down: bfloat16 [32, 2048, 16], P('dp'), may hold values from -0.125 to 0.125
- adapter_up: bfloat16 [32, 16, 2048], P('dp'), may hold values from -1.5 to 1.5
- head_weight: bfloat16 [2048, 65536], P(None, ('dp', 'tensor')), may hold values from -0.375 to 0.375
Outputs:
- sublayer_out: bfloat16 [16384, 2048], P(('dp', 'tensor'))
- last_norm: float32 [24], replicated
- block_logit: float32 [24, 32], P(None, 'tensor')
Inputs may be any that keep to these rules, and one draw needn't show every extreme that they name: `routes`: in each aligned block of 128 rows (the rows of one device), no expert is named by more than 32 rows, a bound that some block reaches. The lengths sum to 16384; the largest is exactly 1920. Each position of the store appears once: adapter a is stored at position adapter_slot[a] of adapter_down and adapter_up.
All inputs are finite; a program needn't handle non-finite values.
Results may differ from a plain program's by a relative error of at most 0.0066.
Values may be sent and summed in bfloat16 or wider, within the bound.
A program may use at most 128 MiB of HBM per device.

v0:
```python
import jax
import jax.numpy as jnp
from jax import lax
from jax.sharding import PartitionSpec as P

CAP = 32


def apply_norm(tokens, norm_gain):
    values = tokens.astype(jnp.float32)
    scaled = lax.rsqrt(jnp.mean(values * values, axis=-1, keepdims=True) + 1e-06)
    return (values * scaled * norm_gain.astype(jnp.float32)).astype(jnp.bfloat16)


def feed_forward(inputs, gate_mat, up_mat, down_mat):
    gate_portion = jnp.dot(inputs, gate_mat, preferred_element_type=jnp.float32)
    up_part = jnp.dot(inputs, up_mat, preferred_element_type=jnp.float32)
    hidden = (jax.nn.silu(gate_portion) * up_part).astype(jnp.bfloat16)
    return jnp.dot(hidden, down_mat, preferred_element_type=jnp.float32)


def token_slots(positions, lengths, request_adapter, adapter_slot):
    request_ends = jnp.cumsum(lengths)
    request = jnp.sum((request_ends[None, :] <= positions[:, None]).astype(jnp.int32), axis=1)
    request_pick = (
        request[:, None] == jnp.arange(request_adapter.shape[0], dtype=jnp.int32)[None, :]
    )
    adapter = jnp.sum(jnp.where(request_pick, request_adapter[None, :], 0), axis=1)
    adapter_pick = adapter[:, None] == jnp.arange(adapter_slot.shape[0], dtype=jnp.int32)[None, :]
    return jnp.sum(jnp.where(adapter_pick, adapter_slot[None, :], 0), axis=1)


def adapter_delta(inputs, slot_ids, down_store, up_store):
    held_count = down_store.shape[0]
    model_width = down_store.shape[1]
    rank_size = down_store.shape[2]
    flat_down = jnp.transpose(down_store, (1, 0, 2)).reshape(model_width, held_count * rank_size)
    low_rank = jnp.dot(inputs, flat_down, preferred_element_type=jnp.float32)
    low_rank = low_rank.reshape(inputs.shape[0], held_count, rank_size)
    keep_mask = slot_ids[:, None] == jnp.arange(held_count, dtype=jnp.int32)[None, :]
    low_rank = jnp.where(keep_mask[:, :, None], low_rank, 0.0).astype(jnp.bfloat16)
    low_rank = low_rank.reshape(inputs.shape[0], held_count * rank_size)
    flat_up = up_store.reshape(held_count * rank_size, up_store.shape[2])
    return jnp.dot(low_rank, flat_up, preferred_element_type=jnp.float32)


def local(
    tokens,
    norm_gain,
    routes,
    route_gates,
    lengths,
    request_adapter,
    adapter_slot,
    expert_gate,
    expert_up,
    expert_down,
    shared_gate,
    shared_up_weight,
    shared_down,
    adapter_down,
    adapter_up,
    head_weight,
):
    tok_rows = tokens.shape[0]
    model_width = tokens.shape[1]
    route_count = routes.shape[1]
    tensor_size = lax.axis_size("tensor")
    tensor_pos = lax.axis_index("tensor")
    data_pos = lax.axis_index("dp")
    local_experts = expert_gate.shape[0]
    all_experts = local_experts * tensor_size
    slot_range = jnp.arange(CAP, dtype=jnp.int32)
    normed = apply_norm(tokens, norm_gain)
    numbers = jnp.arange(all_experts, dtype=jnp.int32)
    route_hits = routes[:, :, None] == numbers[None, None, :]
    chosen = jnp.any(route_hits, axis=1)
    weight = jnp.sum(
        jnp.where(route_hits, route_gates[:, :, None], jnp.zeros((), jnp.bfloat16)), axis=1
    )
    slot_place = jnp.cumsum(chosen.astype(jnp.int32), axis=0) - 1
    pooled, pooled_routes = (
        lax.all_gather(normed, "tensor", axis=0, tiled=True),
        lax.all_gather(routes.astype(jnp.bfloat16), "tensor", axis=0, tiled=True),
    )
    pooled = pooled.reshape(tensor_size, tok_rows, model_width)
    source_routes = pooled_routes.astype(jnp.int32).reshape(tensor_size, tok_rows, route_count)
    own_numbers = tensor_pos * local_experts + jnp.arange(local_experts, dtype=jnp.int32)
    source_hits = source_routes[:, :, :, None] == own_numbers[None, None, None, :]
    source_chosen = jnp.any(source_hits, axis=2)
    source_place = jnp.cumsum(source_chosen.astype(jnp.int32), axis=1) - 1
    source_pick = source_chosen[:, :, :, None] & (
        source_place[:, :, :, None] == slot_range[None, None, None, :]
    )
    source_pick = jnp.where(source_pick, 1.0, 0.0).astype(jnp.bfloat16)
    incoming = jnp.einsum(
        "sijc,sid->sjcd", source_pick, pooled, preferred_element_type=jnp.float32
    ).astype(jnp.bfloat16)
    gate_portion = jnp.einsum(
        "secd,edf->secf", incoming, expert_gate, preferred_element_type=jnp.float32
    )
    up_part = jnp.einsum("secd,edf->secf", incoming, expert_up, preferred_element_type=jnp.float32)
    hidden = (jax.nn.silu(gate_portion) * up_part).astype(jnp.bfloat16)
    expert_out = jnp.einsum(
        "secf,efd->secd", hidden, expert_down, preferred_element_type=jnp.float32
    ).astype(jnp.bfloat16)
    returned_rows = lax.all_to_all(expert_out, "tensor", split_axis=0, concat_axis=0, tiled=True)
    returned_rows = returned_rows.reshape(all_experts, CAP, model_width)
    mixing_result = jnp.where(
        slot_place[:, :, None] == slot_range[None, None, :],
        weight[:, :, None],
        jnp.zeros((), jnp.bfloat16),
    )
    routed_output = jnp.einsum(
        "kbt,btw->kw", mixing_result, returned_rows, preferred_element_type=jnp.float32
    )
    own_base = (data_pos * tensor_size + tensor_pos) * tok_rows
    own_positions = own_base + jnp.arange(tok_rows, dtype=jnp.int32)
    peer_rows = lax.all_gather(normed, "dp", axis=0, tiled=True)
    shared_sum = lax.psum_scatter(
        feed_forward(peer_rows, shared_gate, shared_up_weight, shared_down),
        "dp",
        scatter_dimension=0,
        tiled=True,
    )
    own_slots = token_slots(own_positions, lengths, request_adapter, adapter_slot)
    store_down, store_up = (
        lax.all_gather(adapter_down, "dp", axis=0, tiled=True),
        lax.all_gather(adapter_up, "dp", axis=0, tiled=True),
    )
    summed = routed_output + shared_sum + adapter_delta(normed, own_slots, store_down, store_up)
    sublayer_out = summed.astype(jnp.bfloat16)
    request_ends = jnp.cumsum(lengths)
    last_pick = jnp.where(request_ends[:, None] - 1 == own_positions[None, :], 1.0, 0.0).astype(
        jnp.bfloat16
    )
    last_part = jnp.dot(last_pick, sublayer_out, preferred_element_type=jnp.float32)
    last_states = lax.psum(last_part, ("dp", "tensor"))
    last_norm = jnp.sqrt(jnp.sum(last_states * last_states, axis=1))
    logits = jnp.dot(
        last_states.astype(jnp.bfloat16), head_weight, preferred_element_type=jnp.float32
    )
    block_logit = lax.pmax(jnp.max(logits, axis=1), "dp")
    return (sublayer_out, last_norm, block_logit[:, None])


def solution(mesh):
    placed = (
        P(("dp", "tensor"), None),
        P(),
        P(("dp", "tensor"), None),
        P(("dp", "tensor"), None),
        P(),
        P(),
        P(),
        P("tensor", None, None),
        P("tensor", None, None),
        P("tensor", None, None),
        P(None, "dp"),
        P(None, "dp"),
        P("dp", None),
        P("dp", None, None),
        P("dp", None, None),
        P(None, ("dp", "tensor")),
    )
    return jax.shard_map(
        local,
        mesh=mesh,
        in_specs=placed,
        out_specs=(P(("dp", "tensor"), None), P(), P(None, "tensor")),
        check_vma=False,
    )
```

profile of v0, /device:TPU:1, one launch (start us, length us, event | category | flops | bytes accessed | tf_op | source)
XLA Modules:
  0.0 400.6 jit_solution(9235097486257809376)
XLA Ops:
  7.2 0.9 convert_element_type.84
  8.1 1.3 fusion.41
  9.4 2.0 fusion.43
  12.3 33.4 %all-gather.7.cloned.1.call-done = bf16[512,2048]{1,0:T(8,128)(2,1)} async-done(((bf16[128,2048]{1,0:T(8,128)(2,1)}), bf16[512,2048]{1,0:T(8,128)(2,1)}) %all-gather.7.cloned.1.call-update) | async-done | bytes 2097168 | tf_op jit(solution)/shard_map/all_gather | solution.py:119
  45.6 3.8 fusion.82
  49.4 6.3 %fusion.32 = f32[512,2048]{1,0:T(8,128)} fusion(bf16[352,2048]{1,0:T(8,128)(2,1)S(1)} %copy-done.8, bf16[512,2048]{1,0:T(8,128)(2,1)} %all-gather.7.cloned.1.call-done, bf16[2048,352]{0,1:T(8,128)(2,1)} %param.27, f32[512,352]{0,1:T(8,128)} %fusion.82), kind=kOutput, calls=%fused_computation.29 | convolution fusion | flops 1477476352 | bytes 9895936 | tf_op jit(solution)/shard_map/dot_general | solution.py:19
  55.8 1.0 copy-done.4
  56.8 1.1 copy.47
  57.9 25.1 %all_gather.15 = bf16[4096,6]{0,1:T(8,128)(2,1)S(1)} all-gather(bf16[128,6]{0,1:T(8,128)(2,1)S(1)} %convert_element_type.79), channel_id=1, replica_groups=mesh['dp'=4,'tensor'=32] {'tensor'}, dimensions={0}, use_global_device_ids=true | all-gather | bytes 50688 | tf_op jit(solution)/shard_map/all_gather | solution.py:84
  83.4 38.2 %all-gather.5.cloned.1.call-done = bf16[4096,2048]{1,0:T(8,128)(2,1)} async-done(((bf16[128,2048]{1,0:T(8,128)(2,1)}), bf16[4096,2048]{1,0:T(8,128)(2,1)}) %all-gather.5.cloned.1.call-update) | async-done | bytes 16777232 | tf_op jit(solution)/shard_map/all_gather | solution.py:83
  121.6 8.1 %convolution_convert_fusion = bf16[32,32,2048]{2,1,0:T(8,128)(2,1)S(1)} fusion(bf16[32,128,2048]{2,1,0:T(8,128)(2,1)} %bitcast.109, s32[32,128]{1,0:T(8,128)S(1)} %broadcast_add_fusion.1, pred[32,128]{1,0:T(8,128)(4,1)S(1)} %bitcast.111), kind=kOutput, calls=%fused_computation.16 | convolution fusion | flops 539492352 | bytes 20992000 | tf_op jit(solution)/shard_map/sijc,sid->sjcd/dot_general | solution.py:96
  129.7 2.1 copy-done.1
  131.8 10.6 %fusion.3 = f32[32,32,1408]{2,1,0:T(8,128)} fusion(bf16[32,32,2048]{2,1,0:T(8,128)(2,1)S(1)} %convolution_convert_fusion, bf16[1,2048,1408]{2,1,0:T(8,128)(2,1)} %param.24), kind=kOutput, calls=%fused_computation.4 | convolution fusion | flops 5905580032 | bytes 15728640 | tf_op jit(solution)/shard_map/secd,edf->secf/dot_general | solution.py:102
  142.4 21.1 %convert_bitcast_fusion = bf16[32,1,32,2048]{3,2,1,0:T(8,128)(2,1)} fusion(bf16[1,1408,2048]{2,1,0:T(8,128)(2,1)} %param.25, f32[32,32,1408]{2,1,0:T(8,128)} %fusion.3, bf16[32,32,2048]{2,1,0:T(8,128)(2,1)} %copy-done.1, bf16[1,2048,1408]{2,1,0:T(8,128)(2,1)} %param.23), kind=kOutput, calls=%fused_computation.15 | convolution fusion | flops 11821907968 | bytes 25690112 | tf_op jit(solution)/shard_map/secf,efd->secd/dot_general | solution.py:104
  163.5 5.2 %all-to-all-start = ((bf16[32,1,32,2048]{3,2,1,0:T(8,128)(2,1)}), bf16[32,1,32,2048]{3,2,1,0:T(8,128)(2,1)}, u32[]{:S(2)}, u32[]{:S(2)}) async-start(bf16[32,1,32,2048]{3,2,1,0:T(8,128)(2,1)} %convert_bitcast_fusion), calls=%async_computation | async-start | bytes 8388608 | tf_op jit(solution)/shard_map/all_to_all | solution.py:107
  170.6 50.3 %all-to-all-done = bf16[32,1,32,2048]{3,2,1,0:T(8,128)(2,1)} async-done(((bf16[32,1,32,2048]{3,2,1,0:T(8,128)(2,1)}), bf16[32,1,32,2048]{3,2,1,0:T(8,128)(2,1)}, u32[]{:S(2)}, u32[]{:S(2)}) %all-to-all-start) | async-done | bytes 4194336 | tf_op jit(solution)/shard_map/all_to_all | solution.py:107
  220.9 4.3 %fusion.23 = f32[128,2048]{1,0:T(8,128)} fusion(f32[128,2048]{1,0:T(8,128)} %reduce-scatter.2.cloned.1.call-done, bf16[32,1,32,2048]{3,2,1,0:T(8,128)(2,1)} %all-to-all-done, s32[128,32]{0,1:T(8,128)S(1)} %copy.43, bf16[128,32]{0,1:T(8,128)(2,1)S(1)} %fusion.68), kind=kOutput, calls=%fused_computation.21 | convolution fusion | flops 537395200 | bytes 6316032 | tf_op jit(solution)/shard_map/kbt,btw->kw/dot_general | solution.py:114
  225.2 9.3 %all-gather.9.cloned.1.call-done = bf16[32,2048,16]{1,2,0:T(8,128)(2,1)} async-done(((bf16[8,2048,16]{1,2,0:T(8,128)(2,1)}), bf16[32,2048,16]{1,2,0:T(8,128)(2,1)}) %all-gather.9.cloned.1.call-update) | async-done | bytes 2097168 | tf_op jit(solution)/shard_map/all_gather | solution.py:128
  234.5 4.5 %fusion.26 = bf16[128,2048]{1,0:T(8,128)(2,1)S(1)} fusion(f32[128,2048]{1,0:T(8,128)} %fusion.23, bf16[32,16,2048]{2,0,1:T(8,128)(2,1)} %all-gather.11.cloned.1.call-done, bf16[32,16,2048]{2,1,0:T(8,128)(2,1)} %bitcast.110, bf16[128,2048]{1,0:T(8,128)(2,1)S(1)} %copy-done.2, pred[128,32]{0,1:T(8,128)(4,1)S(1)} %iota_compare_fusion.3), kind=kOutput, calls=%fused_computation.22 | convolution fusion | flops 537526272 | bytes 6295552 | tf_op jit(solution)/shard_map/dot_general | solution.py:44
  239.0 0.9 fusion.69
  240.0 142.9 %all-reduce.2.cloned.1.call-done = f32[24,2048]{1,0:T(8,128)} async-done(((f32[24,2048]{1,0:T(8,128)}), f32[24,2048]{1,0:T(8,128)}) %all-reduce.2.cloned.1.call-update) | async-done | bytes 196624 | tf_op jit(solution)/shard_map/psum | solution.py:138
  382.8 1.4 convolution_reduce_fusion
  384.2 7.9 %pmax.7 = f32[24,1]{0,1:T(1,128)} all-reduce(f32[24,1]{0,1:T(1,128)S(1)} %bitcast.112), channel_id=1, replica_groups=mesh['dp'=4,'tensor'=32] {'dp'}, use_global_device_ids=true, to_apply=%region_14.15 | all-reduce | flops 24 | bytes 192 | tf_op jit(solution)/shard_map/pmax | solution.py:143
  392.2 1.1 multiply_reduce_fusion
  (57 shorter events, 3.7 us)
Async XLA Ops:
  7.2 375.7 %copy-start = (bf16[2048,512]{1,0:T(8,128)(2,1)S(1)}, bf16[2048,512]{1,0:T(8,128)(2,1)}, u32[]{:S(2)}) copy-start(bf16[2048,512]{1,0:T(8,128)(2,1)} %param.31) | copy-start | bytes 6291460
  7.2 42.2 %copy-start.8 = (bf16[352,2048]{1,0:T(8,128)(2,1)S(1)}, bf16[352,2048]{1,0:T(8,128)(2,1)}, u32[]{:S(2)}) copy-start(bf16[352,2048]{1,0:T(8,128)(2,1)} %param.28) | copy-start | bytes 4325380
  7.2 38.4 %all-gather.7.cloned.1.call-start = ((), (), s32[]{:S(2)}) async-start(), calls=%async_computation.3 | async-start | bytes 2621440 | tf_op jit(solution)/shard_map/all_gather | solution.py:119
  11.5 110.1 %all-gather.5.cloned.1.call-start = ((), (), s32[]{:S(2)}) async-start(), calls=%async_computation.2 | async-start | bytes 17301504 | tf_op jit(solution)/shard_map/all_gather | solution.py:83
  12.2 158.4 %reduce-scatter.2.cloned.1.call-start = ((), (), s32[]{:S(2)}) async-start(), calls=%async_computation.4 | async-start | bytes 5242880 | tf_op jit(solution)/shard_map/reduce_scatter | solution.py:120
  55.7 1.0 copy-start.4
  55.7 2.1 copy-start.5
  55.8 169.5 %all-gather.11.cloned.1.call-start = ((), (), s32[]{:S(2)}) async-start(), calls=%async_computation.6 | async-start | bytes 2621440 | tf_op jit(solution)/shard_map/all_gather | solution.py:129
  129.7 2.1 copy-start.1
  163.5 6.5 %copy-start.7 = (s32[24]{0:T(128)S(1)}, s32[24]{0:T(128)}, u32[]{:S(2)}) copy-start(s32[24]{0:T(128)} %param.20) | copy-start | bytes 292
  163.5 6.9 %copy-start.9 = (s32[24]{0:T(128)S(1)}, s32[24]{0:T(128)}, u32[]{:S(2)}) copy-start(s32[24]{0:T(128)} %param.21) | copy-start | bytes 292
  163.5 7.0 %copy-start.10 = (s32[32]{0:T(128)S(1)}, s32[32]{0:T(128)}, u32[]{:S(2)}) copy-start(s32[32]{0:T(128)} %param.22) | copy-start | bytes 388
  163.5 7.0 %copy-start.6 = (bf16[128,6]{0,1:T(8,128)(2,1)S(1)}, bf16[128,6]{0,1:T(8,128)(2,1)}, u32[]{:S(2)}) copy-start(bf16[128,6]{0,1:T(8,128)(2,1)} %param.19) | copy-start | bytes 4612
  163.5 57.4 %all-to-all-start = ((bf16[32,1,32,2048]{3,2,1,0:T(8,128)(2,1)}), bf16[32,1,32,2048]{3,2,1,0:T(8,128)(2,1)}, u32[]{:S(2)}, u32[]{:S(2)}) async-start(bf16[32,1,32,2048]{3,2,1,0:T(8,128)(2,1)} %convert_bitcast_fusion), calls=%async_computation | async-start | bytes 8388608 | tf_op jit(solution)/shard_map/all_to_all | solution.py:107
  168.7 65.8 %copy-start.2 = (bf16[128,2048]{1,0:T(8,128)(2,1)S(1)}, bf16[128,2048]{1,0:T(8,128)(2,1)}, u32[]{:S(2)}) copy-start(bf16[128,2048]{1,0:T(8,128)(2,1)} %fusion.43) | copy-start | bytes 1572868
  168.7 65.7 %all-gather.9.cloned.1.call-start = ((), (), s32[]{:S(2)}) async-start(), calls=%async_computation.5 | async-start | bytes 2621440 | tf_op jit(solution)/shard_map/all_gather | solution.py:128
  169.3 213.5 %all-reduce.2.cloned.1.call-start = ((), (), s32[]{:S(2)}) async-start(), calls=%async_computation.7 | async-start | bytes 393216 | tf_op jit(solution)/shard_map/psum | solution.py:138
  239.0 154.7 %copy-start.3 = (bf16[128,2048]{1,0:T(8,128)(2,1)}, bf16[128,2048]{1,0:T(8,128)(2,1)S(1)}, u32[]{:S(2)}) copy-start(bf16[128,2048]{1,0:T(8,128)(2,1)S(1)} %fusion.26) | copy-start | bytes 1572868
Sparse Core Ops, SparseCore 0:
  11.6 34.0 all-gather.6
  48.5 73.0 all-gather.4
  124.0 45.7 reduce-scatter.1
  171.4 30.4 all-gather.10
  203.6 30.8 all-gather.8
  240.1 142.6 all-reduce.1
where the time goes:
time: 402 us; the launch traced here: 401 us
  waiting for transfers between devices  275 us (68%)
  matrix products  61 us (15%)
  blocking collectives  33 us (8%)
  between operations  14.3 us (4%)
  other arithmetic  6.28 us (2%)
  starting transfers between devices  5.68 us (1%)
  local copies, waits for them, and re-layouts  4.94 us (1%)
    psum x1, waiting for transfers between devices, local(): last_states = lax.psum(last_part, ('dp', 'tensor'))  143 us
    all_to_all x1, waiting for transfers between devices, local(): lax.all_to_all(expert_out, 'tensor', split_axis=0, concat_axis=0, tiled=T...  50.3 us
    all_gather x1, waiting for transfers between devices, local(): lax.all_gather(normed, 'tensor', axis=0, tiled=True)  38.2 us
    all_gather x1, waiting for transfers between devices, local(): peer_rows = lax.all_gather(normed, 'dp', axis=0, tiled=True)  33.4 us
    all_gather x1, blocking collectives, local(): lax.all_gather(routes.astype(jnp.bfloat16), 'tensor', axis=0, tiled=True)  25.1 us
    dot_general x1, matrix products, local(): jnp.einsum('secf,efd->secd', hidden, expert_down, preferred_element_type=...  21.1 us
    dot_general x1, matrix products, local(): jnp.einsum('secd,edf->secf', incoming, expert_up, preferred_element_type=...  10.6 us
    all_gather x1, waiting for transfers between devices, local(): lax.all_gather(adapter_down, 'dp', axis=0, tiled=True)  9.27 us
  transfers between devices with their start and end apart: 7, of which 5 were waited for; matrix products, arithmetic and copies ran while one was open for 14% of the time, Pallas kernels for 0%

commit v1 on v0

v1 whole, which is shorter than its diff:
```python
import functools

import jax
import jax.numpy as jnp
from jax import lax
from jax.experimental import pallas as pl
from jax.experimental.pallas import tpu as pltpu
from jax.sharding import PartitionSpec as P

CAP = 32
HOPS = (0, 1, 3, 2)
PAD_ROWS = 32
F32 = jnp.float32
BF16 = jnp.bfloat16
MESH = pl.DeviceIdType.MESH


def body(
    lengths,
    request_adapter,
    adapter_slot,
    tokens,
    gain,
    meta_in,
    expert_gate,
    expert_up,
    expert_down,
    shared_gate,
    shared_up,
    shared_down,
    low_down,
    low_up,
    head,
    out,
    norm_out,
    logit_out,
    w_gate,
    w_up,
    w_down,
    w_sgate,
    w_sup,
    w_sdown,
    w_ldown,
    w_lup,
    w_head,
    first_rows,
    peer_rows,
    meta,
    picked,
    arrived,
    results,
    returned,
    mixing,
    hidden,
    part_send,
    part_recv,
    shared_send,
    shared_recv,
    total,
    slot_grid,
    last_mine,
    last_core,
    last_sum,
    last_recv,
    last_full,
    top_mine,
    top_recv,
    load_sem,
    meta_send_sem,
    meta_recv_sem,
    first_send_sem,
    first_recv_sem,
    peer_send_sem,
    peer_recv_sem,
    pick_send_sem,
    pick_recv_sem,
    ret_send_sem,
    ret_recv_sem,
    part_send_sem,
    part_recv_sem,
    shared_send_sem,
    shared_recv_sem,
    core_send_sem,
    core_recv_sem,
    last_send_sem,
    last_recv_sem,
    top_send_sem,
    top_recv_sem,
):
    width = tokens.shape[1]
    rows = tokens.shape[0]
    d = lax.axis_index("dp")
    t = lax.axis_index("tensor")
    y = t // 8
    z = (t // 2) % 4
    c = t % 2
    one = c == 1

    def at(ty, tz, tc):
        return (d, ty * 8 + tz * 2 + tc)

    def along_first(k):
        return at(
            jnp.where(one, y, (y + k) % 4),
            jnp.where(one, (z + k) % 4, z),
            c,
        )

    def along_x(k):
        return ((d + k) % 4, t)

    def expert_of(j):
        return jnp.where(one, (j // 2) * 8 + z * 2 + j % 2, y * 8 + j)

    own_j = jnp.where(one, y * 2 + 1, z * 2)
    own_q = jnp.where(one, 4 + y, z)

    def relay_of(q):
        return jnp.where(q < 4, y * 8 + q * 2, (q - 4) * 8 + z * 2 + 1)

    loads = []
    for i, (src, dst) in enumerate(
        (
            (shared_gate, w_sgate),
            (shared_up, w_sup),
            (low_down, w_ldown),
            (shared_down, w_sdown),
            (low_up, w_lup),
            (expert_gate.at[0], w_gate),
            (expert_up.at[0], w_up),
            (expert_down.at[0], w_down),
            (head, w_head),
        )
    ):
        loads.append(pltpu.make_async_copy(src, dst, load_sem.at[i]))
    for load in loads:
        load.start()

    barrier = pltpu.get_barrier_semaphore()
    greeted = [at(y, z, 1 - c)]
    for k in (1, 2, 3):
        for o in (0, 1):
            greeted.append(at(y, (z + k) % 4, o))
            greeted.append(at((y + k) % 4, z, o))
        greeted.append(along_x(k))
    for target in greeted:
        pl.semaphore_signal(barrier, inc=1, device_id=target, device_id_type=MESH)

    values = tokens[...].astype(F32)
    scaled = lax.rsqrt(jnp.mean(values * values, axis=-1, keepdims=True) + 1e-06)
    normed = (values * scaled * gain[...].astype(F32)).astype(BF16)
    first_rows[0] = normed
    peer_rows[0] = normed
    meta[0] = meta_in[...]

    lane = lax.broadcasted_iota(jnp.int32, (8, rows), 1)
    row = lax.broadcasted_iota(jnp.int32, (8, rows), 0)
    hop = jnp.where(row == 2, 3, jnp.where(row == 3, 2, row))
    place = (((d - hop + 8) % 4) * 32 + t) * rows + lane
    slots = jnp.zeros((8, rows), jnp.int32)
    pick_at = lax.broadcasted_iota(jnp.int32, (PAD_ROWS, rows), 0)
    own_place = (d * 32 + t) * rows + lax.broadcasted_iota(jnp.int32, (PAD_ROWS, rows), 1)
    last_pick = jnp.zeros((PAD_ROWS, rows), F32)
    start = jnp.int32(0)
    for r in range(lengths.shape[0]):
        slot = adapter_slot[request_adapter[r]]
        slots = jnp.where(place >= start, slot, slots)
        start = start + lengths[r]
        last_pick = jnp.where((pick_at == r) & (own_place == start - 1), 1.0, last_pick)
    slots = slots.astype(F32)
    for p in range(4):
        slot_grid[p] = jnp.transpose(jnp.broadcast_to(slots[p : p + 1], (rows, rows)))

    pl.semaphore_wait(barrier, len(greeted))

    def meta_copy(p):
        return pltpu.make_async_remote_copy(
            src_ref=meta.at[0],
            dst_ref=meta.at[p],
            send_sem=meta_send_sem.at[p],
            recv_sem=meta_recv_sem.at[p],
            device_id=along_first(HOPS[p]),
            device_id_type=MESH,
        )

    def first_copy(p):
        return pltpu.make_async_remote_copy(
            src_ref=first_rows.at[0],
            dst_ref=first_rows.at[p],
            send_sem=first_send_sem.at[p],
            recv_sem=first_recv_sem.at[p],
            device_id=along_first(HOPS[p]),
            device_id_type=MESH,
        )

    def peer_copy(p):
        return pltpu.make_async_remote_copy(
            src_ref=peer_rows.at[0],
            dst_ref=peer_rows.at[p],
            send_sem=peer_send_sem.at[p],
            recv_sem=peer_recv_sem.at[p],
            device_id=along_x(HOPS[p]),
            device_id_type=MESH,
        )

    for p in (1, 2, 3):
        meta_copy(p).start()
        first_copy(p).start()
    for p in (1, 2, 3):
        peer_copy(p).start()

    def pick_copy(p, j):
        return pltpu.make_async_remote_copy(
            src_ref=picked.at[p, j],
            dst_ref=arrived.at[p, own_q],
            send_sem=pick_send_sem.at[p, j],
            recv_sem=pick_recv_sem.at[p, own_q],
            device_id=(d, expert_of(j)),
            device_id_type=MESH,
        )

    def pick_wait(p, q):
        return pltpu.make_async_remote_copy(
            src_ref=picked.at[p, own_j],
            dst_ref=arrived.at[p, q],
            send_sem=pick_send_sem.at[p, own_j],
            recv_sem=pick_recv_sem.at[p, q],
            device_id=(d, relay_of(q)),
            device_id_type=MESH,
        )

    def own_at(q):
        return jnp.where(q < 4, z * 2 + c, y * 2 + c)

    def ret_copy(p, q):
        return pltpu.make_async_remote_copy(
            src_ref=results.at[p, q],
            dst_ref=returned.at[p, own_at(q)],
            send_sem=ret_send_sem.at[p, q],
            recv_sem=ret_recv_sem.at[p, own_at(q)],
            device_id=(d, relay_of(q)),
            device_id_type=MESH,
        )

    def ret_wait(p, j):
        return pltpu.make_async_remote_copy(
            src_ref=results.at[p, own_q],
            dst_ref=returned.at[p, j],
            send_sem=ret_send_sem.at[p, own_q],
            recv_sem=ret_recv_sem.at[p, j],
            device_id=(d, expert_of(j)),
            device_id_type=MESH,
        )

    def other_j(r):
        near = ((1, 0), (3, 0), (1, 1), (3, 1), (2, 0), (2, 1), (0, 1))[r]
        return ((own_j // 2 + near[0]) % 4) * 2 + (c + near[1]) % 2

    def other_q(r):
        return (own_q + r + 1) % 8

    tri_a = lax.broadcasted_iota(jnp.int32, (rows, rows), 0)
    tri_b = lax.broadcasted_iota(jnp.int32, (rows, rows), 1)
    upper = jnp.where(tri_a <= tri_b, 1.0, 0.0).astype(F32)
    index_j = lax.broadcasted_iota(jnp.int32, (8, rows), 0)
    wanted = expert_of(index_j).astype(F32)
    slot_index = lax.broadcasted_iota(jnp.int32, (8, CAP, rows), 1).astype(F32)

    def select(p):
        table = meta[p]
        chosen = jnp.zeros((8, rows), F32)
        weight = jnp.zeros((8, rows), F32)
        for k in range(6):
            same = table[k : k + 1, :] == wanted
            chosen = jnp.where(same, 1.0, chosen)
            weight = jnp.where(same, table[8 + k : 9 + k, :], weight)
        count = jnp.dot(chosen, upper, preferred_element_type=F32)
        slot_of = jnp.where(chosen > 0.5, count - 1.0, -1.0)
        hit = jnp.broadcast_to(slot_of[:, None, :], (8, CAP, rows)) == slot_index
        pick = jnp.where(hit, 1.0, 0.0).reshape(8 * CAP, rows).astype(BF16)
        mix = jnp.where(hit, jnp.broadcast_to(weight[:, None, :], (8, CAP, rows)), 0.0)
        mixing[p] = jnp.transpose(mix.reshape(8 * CAP, rows)).astype(BF16)

        def columns(n, carry):
            cols = pl.ds(pl.multiple_of(n * 512, 512), 512)
            got = jnp.dot(pick, first_rows[p, :, cols], preferred_element_type=F32)
            picked[p, :, :, cols] = got.astype(BF16).reshape(8, CAP, 512)
            return carry

        lax.fori_loop(0, width // 512, columns, 0)
        arrived[p, own_q] = picked[p, own_j]
        for r in range(7):
            pick_copy(p, other_j(r)).start()

    def shared(b):
        at_b = pl.ds(b * 2, 2)
        x = peer_rows[at_b].reshape(2 * rows, width)
        gate_part = jnp.dot(x, w_sgate[...], preferred_element_type=F32)
        up_part = jnp.dot(x, w_sup[...], preferred_element_type=F32)
        inner = (gate_part / (1.0 + jnp.exp(-gate_part)) * up_part).astype(BF16)
        low = jnp.dot(x, w_ldown[...], preferred_element_type=F32)
        lanes = lax.broadcasted_iota(jnp.int32, low.shape, 1) // 16 + d * 8
        keep = slot_grid[at_b].reshape(2 * rows, rows) == lanes.astype(F32)
        low = jnp.where(keep, low, 0.0).astype(BF16)

        def columns(n, carry):
            cols = pl.ds(pl.multiple_of(n * 512, 512), 512)
            part = jnp.dot(inner, w_sdown[:, cols], preferred_element_type=F32)
            part = part + jnp.dot(low, w_lup[:, cols], preferred_element_type=F32)
            shared_send[at_b, :, cols] = part.astype(BF16).reshape(2, rows, 512)

            @pl.when(b == 0)
            def _():
                total[:, cols] = part[:rows]

            return carry

        lax.fori_loop(0, width // 512, columns, 0)

    def shared_copy(p):
        return pltpu.make_async_remote_copy(
            src_ref=shared_send.at[p],
            dst_ref=shared_recv.at[p],
            send_sem=shared_send_sem.at[p],
            recv_sem=shared_recv_sem.at[p],
            device_id=along_x(4 - HOPS[p]),
            device_id_type=MESH,
        )

    def part_copy(p, hop):
        return pltpu.make_async_remote_copy(
            src_ref=part_send.at[p],
            dst_ref=part_recv.at[p],
            send_sem=part_send_sem.at[p],
            recv_sem=part_recv_sem.at[p],
            device_id=along_first(4 - hop),
            device_id_type=MESH,
        )

    inner_width = w_gate.shape[1]
    wide = inner_width // 256

    def gated(p, cols):
        x = arrived[p].reshape(8 * CAP, width)
        gate_part = jnp.dot(x, w_gate[:, cols], preferred_element_type=F32)
        up_part = jnp.dot(x, w_up[:, cols], preferred_element_type=F32)
        act = gate_part / (1.0 + jnp.exp(-gate_part)) * up_part
        hidden[:, cols] = act.astype(BF16)

    def expert(p):
        for r in range(7):
            pick_wait(p, other_q(r)).wait_recv()

        def columns(n, carry):
            gated(p, pl.ds(pl.multiple_of(n * 256, 256), 256))
            return carry

        lax.fori_loop(0, wide, columns, 0)
        if inner_width > wide * 256:
            gated(p, pl.ds(wide * 256, inner_width - wide * 256))

        def down(n, carry):
            cols = pl.ds(pl.multiple_of(n * 512, 512), 512)
            got = jnp.dot(hidden[...], w_down[:, cols], preferred_element_type=F32)
            results[p, :, :, cols] = got.astype(BF16).reshape(8, CAP, 512)
            return carry

        lax.fori_loop(0, width // 512, down, 0)
        returned[p, own_j] = results[p, own_q]
        for r in range(7):
            ret_copy(p, other_q(r)).start()

    def combine(p, own):
        for r in range(7):
            ret_wait(p, other_j(r)).wait_recv()

        def columns(n, carry):
            cols = pl.ds(pl.multiple_of(n * 512, 512), 512)
            got = jnp.dot(
                mixing[p],
                returned[p, :, :, cols].reshape(8 * CAP, 512),
                preferred_element_type=F32,
            )
            if own:
                total[:, cols] += got
            else:
                part_send[p, :, cols] = got.astype(BF16)
            return carry

        lax.fori_loop(0, width // 512, columns, 0)

    def select_step(p, carry):
        @pl.when(p > 0)
        def _():
            pltpu.make_async_remote_copy(
                src_ref=meta.at[0],
                dst_ref=meta.at[p],
                send_sem=meta_send_sem.at[p],
                recv_sem=meta_recv_sem.at[p],
                device_id=along_first(1),
                device_id_type=MESH,
            ).wait_recv()
            pltpu.make_async_remote_copy(
                src_ref=first_rows.at[0],
                dst_ref=first_rows.at[p],
                send_sem=first_send_sem.at[p],
                recv_sem=first_recv_sem.at[p],
                device_id=along_first(1),
                device_id_type=MESH,
            ).wait_recv()

        select(p)
        return carry

    lax.fori_loop(0, 4, select_step, 0)

    for load in loads[:5]:
        load.wait()
    peer_copy(1).wait_recv()

    def shared_step(b, carry):
        @pl.when(b == 1)
        def _():
            peer_copy(2).wait_recv()
            peer_copy(3).wait_recv()

        shared(b)
        return carry

    for load in loads[5:8]:
        load.wait()

    def expert_step(p, carry):
        expert(p)

        @pl.when(p < 2)
        def _():
            shared_step(p, 0)

            @pl.when(p == 0)
            def _():
                shared_copy(1).start()

            @pl.when(p == 1)
            def _():
                shared_copy(2).start()
                shared_copy(3).start()

        return carry

    lax.fori_loop(0, 4, expert_step, 0)
    combine(0, True)

    def combine_step(p, carry):
        combine(p, False)
        part_copy(p, jnp.where(p == 2, 3, jnp.where(p == 3, 2, p))).start()
        return carry

    lax.fori_loop(1, 4, combine_step, 0)

    for p in (1, 2, 3):
        shared_copy(p).wait_recv()
    for p in (1, 2, 3):
        part_copy(p, HOPS[p]).wait_recv()

    def finish(n, carry):
        cols = pl.ds(pl.multiple_of(n * 512, 512), 512)
        value = total[:, cols]
        for p in (1, 2, 3):
            value = value + shared_recv[p, :, cols].astype(F32)
            value = value + part_recv[p, :, cols].astype(F32)
        out[:, cols] = value.astype(BF16)
        return carry

    lax.fori_loop(0, width // 512, finish, 0)

    half = width // 2
    pick_last = last_pick.astype(BF16)
    for h in (0, 1):
        mine = jnp.dot(pick_last, out[:, h * half : (h + 1) * half], preferred_element_type=F32)
        last_mine[h] = mine.astype(BF16)

    def core_copy(i, src, dst):
        return pltpu.make_async_remote_copy(
            src_ref=src,
            dst_ref=dst,
            send_sem=core_send_sem.at[i],
            recv_sem=core_recv_sem.at[i],
            device_id=at(y, z, 1 - c),
            device_id_type=MESH,
        )

    swap = core_copy(0, last_mine.at[1 - c], last_core)
    swap.start()
    swap.wait_recv()
    last_sum[0] = (last_mine[c].astype(F32) + last_core[...].astype(F32)).astype(BF16)
    stage_copies = []
    for a in range(3):
        copies = []
        for k in (1, 3, 2):
            target = (at(y, (z + k) % 4, c), at((y + k) % 4, z, c), along_x(k))[a]
            copies.append(
                pltpu.make_async_remote_copy(
                    src_ref=last_sum.at[a],
                    dst_ref=last_recv.at[a, k],
                    send_sem=last_send_sem.at[a, k],
                    recv_sem=last_recv_sem.at[a, k],
                    device_id=target,
                    device_id_type=MESH,
                )
            )
        for copy in copies:
            copy.start()
        for copy in copies:
            copy.wait_recv()
        value = last_sum[a].astype(F32)
        for k in (1, 2, 3):
            value = value + last_recv[a, k].astype(F32)
        last_sum[a + 1] = value.astype(BF16)
        stage_copies += copies
    last_full[c] = last_sum[3]
    spread = core_copy(1, last_sum.at[3], last_full.at[c])
    spread.start()
    loads[8].wait()
    spread.wait_recv()

    square = jnp.zeros((PAD_ROWS, 1), F32)
    logits = jnp.zeros((PAD_ROWS, w_head.shape[1]), F32)
    for h in (0, 1):
        value = last_full[h]
        wide_value = value.astype(F32)
        square = square + jnp.sum(wide_value * wide_value, axis=1, keepdims=True)
        logits = logits + jnp.dot(
            value, w_head[h * half : (h + 1) * half, :], preferred_element_type=F32
        )
    norm_out[...] = jnp.sqrt(square)[: norm_out.shape[0]]
    best = jnp.max(logits, axis=1, keepdims=True)
    top_mine[...] = jnp.broadcast_to(best, top_mine.shape)
    top_copies = []
    for k in (1, 3, 2):
        top_copies.append(
            pltpu.make_async_remote_copy(
                src_ref=top_mine,
                dst_ref=top_recv.at[k],
                send_sem=top_send_sem.at[k],
                recv_sem=top_recv_sem.at[k],
                device_id=along_x(k),
                device_id_type=MESH,
            )
        )
    for copy in top_copies:
        copy.start()
    for copy in top_copies:
        copy.wait_recv()
    best = top_mine[...]
    for k in (1, 2, 3):
        best = jnp.maximum(best, top_recv[k])
    logit_out[...] = best[: logit_out.shape[0], :1]

    for p in (1, 2, 3):
        meta_copy(p).wait_send()
        first_copy(p).wait_send()
        peer_copy(p).wait_send()
        shared_copy(p).wait_send()
        part_copy(p, HOPS[p]).wait_send()

    def drain(p, carry):
        for r in range(7):
            pick_copy(p, other_j(r)).wait_send()
            ret_copy(p, other_q(r)).wait_send()
        return carry

    lax.fori_loop(0, 4, drain, 0)
    swap.wait_send()
    spread.wait_send()
    for copy in stage_copies + top_copies:
        copy.wait_send()


def local(
    tokens,
    norm_gain,
    routes,
    route_gates,
    lengths,
    request_adapter,
    adapter_slot,
    expert_gate,
    expert_up,
    expert_down,
    shared_gate,
    shared_up_weight,
    shared_down,
    adapter_down,
    adapter_up,
    head_weight,
):
    rows, width = tokens.shape
    inner_width = expert_gate.shape[2]
    shared_width = shared_gate.shape[1]
    held, _, rank = adapter_down.shape
    columns = head_weight.shape[1]
    requests = lengths.shape[0]
    meta = jnp.concatenate(
        [
            jnp.pad(routes.astype(F32).T, ((0, 2), (0, 0))),
            jnp.pad(route_gates.astype(F32).T, ((0, 2), (0, 0))),
        ],
        axis=0,
    )
    low_down = jnp.transpose(adapter_down, (1, 0, 2)).reshape(width, held * rank)
    low_up = adapter_up.reshape(held * rank, width)
    vmem = pl.BlockSpec(memory_space=pltpu.VMEM)
    smem = pl.BlockSpec(memory_space=pltpu.SMEM)
    anywhere = pl.BlockSpec(memory_space=pl.ANY)
    dma = pltpu.SemaphoreType.DMA
    half = width // 2
    sublayer, last_norm, block_logit = pl.pallas_call(
        body,
        out_shape=(
            jax.ShapeDtypeStruct((rows, width), BF16),
            jax.ShapeDtypeStruct((requests, 1), F32),
            jax.ShapeDtypeStruct((requests, 1), F32),
        ),
        in_specs=[smem] * 3 + [vmem] * 3 + [anywhere] * 9,
        out_specs=(vmem, vmem, vmem),
        scratch_shapes=[
            pltpu.VMEM((width, inner_width), BF16),
            pltpu.VMEM((width, inner_width), BF16),
            pltpu.VMEM((inner_width, width), BF16),
            pltpu.VMEM((width, shared_width), BF16),
            pltpu.VMEM((width, shared_width), BF16),
            pltpu.VMEM((shared_width, width), BF16),
            pltpu.VMEM((width, held * rank), BF16),
            pltpu.VMEM((held * rank, width), BF16),
            pltpu.VMEM((width, columns), BF16),
            pltpu.VMEM((4, rows, width), BF16),
            pltpu.VMEM((4, rows, width), BF16),
            pltpu.VMEM((4, 16, rows), F32),
            pltpu.VMEM((4, 8, CAP, width), BF16),
            pltpu.VMEM((4, 8, CAP, width), BF16),
            pltpu.VMEM((4, 8, CAP, width), BF16),
            pltpu.VMEM((4, 8, CAP, width), BF16),
            pltpu.VMEM((4, rows, 8 * CAP), BF16),
            pltpu.VMEM((8 * CAP, inner_width), BF16),
            pltpu.VMEM((4, rows, width), BF16),
            pltpu.VMEM((4, rows, width), BF16),
            pltpu.VMEM((4, rows, width), BF16),
            pltpu.VMEM((4, rows, width), BF16),
            pltpu.VMEM((rows, width), F32),
            pltpu.VMEM((4, rows, rows), F32),
            pltpu.VMEM((2, PAD_ROWS, half), BF16),
            pltpu.VMEM((PAD_ROWS, half), BF16),
            pltpu.VMEM((4, PAD_ROWS, half), BF16),
            pltpu.VMEM((3, 4, PAD_ROWS, half), BF16),
            pltpu.VMEM((2, PAD_ROWS, half), BF16),
            pltpu.VMEM((PAD_ROWS, 128), F32),
            pltpu.VMEM((4, PAD_ROWS, 128), F32),
            dma((9,)),
            dma((4,)),
            dma((4,)),
            dma((4,)),
            dma((4,)),
            dma((4,)),
            dma((4,)),
            dma((4, 8)),
            dma((4, 8)),
            dma((4, 8)),
            dma((4, 8)),
            dma((4,)),
            dma((4,)),
            dma((4,)),
            dma((4,)),
            dma((2,)),
            dma((2,)),
            dma((3, 4)),
            dma((3, 4)),
            dma((4,)),
            dma((4,)),
        ],
        compiler_params=pltpu.CompilerParams(
            collective_id=0, has_side_effects=True, vmem_limit_bytes=63 << 20
        ),
        name="sublayer",
    )(
        lengths,
        request_adapter,
        adapter_slot,
        tokens,
        norm_gain.reshape(1, width),
        meta,
        expert_gate,
        expert_up,
        expert_down,
        shared_gate,
        shared_up_weight,
        shared_down,
        low_down,
        low_up,
        head_weight,
    )
    return (sublayer, last_norm.reshape(requests), block_logit)


def solution(mesh):
    placed = (
        P(("dp", "tensor"), None),
        P(),
        P(("dp", "tensor"), None),
        P(("dp", "tensor"), None),
        P(),
        P(),
        P(),
        P("tensor", None, None),
        P("tensor", None, None),
        P("tensor", None, None),
        P(None, "dp"),
        P(None, "dp"),
        P("dp", None),
        P("dp", None, None),
        P("dp", None, None),
        P(None, ("dp", "tensor")),
    )
    return jax.shard_map(
        local,
        mesh=mesh,
        in_specs=placed,
        out_specs=(P(("dp", "tensor"), None), P(), P(None, "tensor")),
        check_vma=False,
    )
```

time: 402 us -> 128 us (0.32)
  waiting for transfers between devices: 275 us -> 0 us
  Pallas kernels: 0 us -> 113 us
  matrix products: 61 us -> 0 us
  blocking collectives: 33 us -> 0 us
  between operations: 14.3 us -> 0.64 us
  local copies, waits for them, and re-layouts: 4.94 us -> 10.8 us
  starting transfers between devices: 5.68 us -> 0 us
    psum x1 -> x0, waiting for transfers between devices: 143 us -> none  [local(): last_states = lax.psum(last_part, ('dp', 'tensor'))]
    pallas_call x0 -> x1, Pallas kernels: none -> 113 us  [local(): pl.pallas_call(body, out_shape=(jax.ShapeDtypeStruct((rows, width), BF16)...]
    all_gather x4 -> x0, waiting for transfers between devices: 80.9 us -> none  [the longest x1 38.2 us: local(): lax.all_gather(normed, 'tensor', axis=0, tiled=True)]
    dot_general x9 -> x0, matrix products: 61 us -> none  [the longest x1 21.1 us: local(): jnp.einsum('secf,efd->secd', hidden, expert_down, preferred_element_type=...]
    all_to_all x1 -> x0, waiting for transfers between devices: 50.3 us -> none  [local(): lax.all_to_all(expert_out, 'tensor', split_axis=0, concat_axis=0, tiled=T...]
    all_gather x1 -> x0, blocking collectives: 25.1 us -> none  [local(): lax.all_gather(routes.astype(jnp.bfloat16), 'tensor', axis=0, tiled=True)]
    pmax x1 -> x0, blocking collectives: 7.91 us -> none  [local(): block_logit = lax.pmax(jnp.max(logits, axis=1), 'dp')]
    all_to_all x1 -> x0, starting transfers between devices: 5.22 us -> none  [local(): lax.all_to_all(expert_out, 'tensor', split_axis=0, concat_axis=0, tiled=T...]
  transfers between devices with their start and end apart: 7 -> 0, of which waited for: 5 -> 0; matrix products, arithmetic and copies ran while one was open for 14% -> 0% of each run, Pallas kernels for 0% -> 0%
where the time goes in v1:
time: 128 us; the launch traced here: 127 us
  Pallas kernels  113 us (88%)
  local copies, waits for them, and re-layouts  10.8 us (8%)
  other arithmetic  3.31 us (3%)
    pallas_call x1, Pallas kernels, local(): pl.pallas_call(body, out_shape=(jax.ShapeDtypeStruct((rows, width), BF16)...  113 us
    unnamed x6, local copies, waits for them, and re-layouts  7.43 us

profile of v1, /device:TPU:1, one launch (start us, length us, event | category | flops | bytes accessed | tf_op | source)
XLA Modules:
  0.0 127.4 jit_solution(1255548277045362596)
XLA Ops:
  0.6 0.7 convert_bitcast_fusion
  1.3 0.7 pad_convert_fusion
  2.0 0.6 select_maximum_fusion.meta_in
  2.6 1.3 %reshape.18.gain = bf16[1,2048]{1,0:T(2,128)(2,1)} reshape(bf16[2048]{0:T(1024)(128)(2,1)} %param.17) | data formatting | bytes 8192 | tf_op jit(solution)/shard_map/reshape | solution.py:690
  3.9 2.0 %copy.25.low_down = bf16[2048,128]{1,0:T(8,128)(2,1)} copy(bf16[2048,128]{0,1:T(8,128)(2,1)} %bitcast.8) | data formatting | bytes 1048576 | tf_op jit(solution)/shard_map/reshape | solution.py:611
  5.9 0.0 copy-start
  5.9 2.7 %copy.23.shared_gate = bf16[2048,352]{1,0:T(8,128)(2,1)} copy(bf16[2048,352]{0,1:T(8,128)(2,1)} %param.26) | data formatting | bytes 2883584 | tf_op args[10]
  8.6 0.0 copy-done
  8.6 1.6 %copy.24.shared_up = bf16[2048,352]{1,0:T(8,128)(2,1)} copy(bf16[2048,352]{0,1:T(8,128)(2,1)S(1)} %copy-done) | data formatting | bytes 2883584 | tf_op args[11]
  10.2 112.7 %sublayer.1 = (bf16[128,2048]{1,0:T(8,128)(2,1)}, f32[24,1]{1,0:T(8,128)}, f32[24,1]{1,0:T(8,128)}) custom-call(s32[24]{0:T(128)} %lengths.1, s32[24]{0:T(128)} %request_adapter.1, s32[32]{0:T(128)} %adapter_slot.1, bf16[128,2048]{1,0:T(8,128)(2,1)} %tokens.1, bf16[1,2048]{1,0:T(2,128)(2,1)} %reshape.18.gain, f32[16,128]{1,0:T(8,128)} %select_maximum_fusion.meta_in, ...), custom_call_target="tpu_custom_call" | custom-call | tf_op jit(solution)/shard_map/sublayer/pallas_call | solution.py:618
  122.9 1.3 %reduce = f32[24]{0:T(128)} reduce(f32[24,1]{1,0:T(8,128)} %get-tuple-element.7, f32[]{:T(128)} %constant.12), dimensions={1}, to_apply=%get-tuple-element.7.reduce_sub_computation | reduce | bytes 196 | tf_op jit(solution)/shard_map/sublayer/pallas_call | solution.py:618
  124.2 1.3 %copy.26 = f32[24,1]{0,1:T(1,128)} copy(f32[24,1]{1,0:T(8,128)} %get-tuple-element.14) | data formatting | bytes 192
  125.5 1.9 %copy.28 = bf16[128,2048]{1,0:T(8,128)(2,1)} copy(bf16[128,2048]{1,0:T(8,128)(2,1)} %get-tuple-element.18) | data formatting | bytes 1048576
Async XLA Ops:
  5.9 2.7 %copy-start = (bf16[2048,352]{0,1:T(8,128)(2,1)S(1)}, bf16[2048,352]{0,1:T(8,128)(2,1)}, u32[]{:S(2)}) copy-start(bf16[2048,352]{0,1:T(8,128)(2,1)} %param.27) | copy-start | bytes 4325380

commit v2 on v1

--- a/solution.py
+++ b/solution.py
@@ -15,13 +15,18 @@
 MESH = pl.DeviceIdType.MESH
 
 
+def dot_rows(a, b):
+    return lax.dot_general(a, b, (((1,), (1,)), ((), ())), preferred_element_type=F32)
+
+
 def body(
     lengths,
     request_adapter,
     adapter_slot,
     tokens,
     gain,
-    meta_in,
+    routes_in,
+    gates_in,
     expert_gate,
     expert_up,
     expert_down,
@@ -148,10 +153,13 @@
 
     values = tokens[...].astype(F32)
     scaled = lax.rsqrt(jnp.mean(values * values, axis=-1, keepdims=True) + 1e-06)
-    normed = (values * scaled * gain[...].astype(F32)).astype(BF16)
+    gains = gain[...].astype(F32).reshape(1, width)
+    normed = (values * scaled * gains).astype(BF16)
     first_rows[0] = normed
     peer_rows[0] = normed
-    meta[0] = meta_in[...]
+    meta[0] = jnp.zeros_like(meta[0])
+    meta[0, 0:6] = routes_in[...].astype(F32)
+    meta[0, 8:14] = gates_in[...].astype(F32)
 
     lane = lax.broadcasted_iota(jnp.int32, (8, rows), 1)
     row = lax.broadcasted_iota(jnp.int32, (8, rows), 0)
@@ -295,10 +303,10 @@
     def shared(b):
         at_b = pl.ds(b * 2, 2)
         x = peer_rows[at_b].reshape(2 * rows, width)
-        gate_part = jnp.dot(x, w_sgate[...], preferred_element_type=F32)
-        up_part = jnp.dot(x, w_sup[...], preferred_element_type=F32)
+        gate_part = dot_rows(x, w_sgate[...])
+        up_part = dot_rows(x, w_sup[...])
         inner = (gate_part / (1.0 + jnp.exp(-gate_part)) * up_part).astype(BF16)
-        low = jnp.dot(x, w_ldown[...], preferred_element_type=F32)
+        low = dot_rows(x, w_ldown[...])
         lanes = lax.broadcasted_iota(jnp.int32, low.shape, 1) // 16 + d * 8
         keep = slot_grid[at_b].reshape(2 * rows, rows) == lanes.astype(F32)
         low = jnp.where(keep, low, 0.0).astype(BF16)
@@ -495,20 +503,23 @@
     swap.wait_recv()
     last_sum[0] = (last_mine[c].astype(F32) + last_core[...].astype(F32)).astype(BF16)
     stage_copies = []
+    third = half // 384 * 128
+    groups = ((0, third), (third, third), (2 * third, half - 2 * third))
     for a in range(3):
         copies = []
         for k in (1, 3, 2):
-            target = (at(y, (z + k) % 4, c), at((y + k) % 4, z, c), along_x(k))[a]
-            copies.append(
-                pltpu.make_async_remote_copy(
-                    src_ref=last_sum.at[a],
-                    dst_ref=last_recv.at[a, k],
-                    send_sem=last_send_sem.at[a, k],
-                    recv_sem=last_recv_sem.at[a, k],
-                    device_id=target,
-                    device_id_type=MESH,
+            for g, (off, size) in enumerate(groups):
+                targets = (at(y, (z + k) % 4, c), at((y + k) % 4, z, c), along_x(k))
+                copies.append(
+                    pltpu.make_async_remote_copy(
+                        src_ref=last_sum.at[a, :, pl.ds(off, size)],
+                        dst_ref=last_recv.at[a, k, :, pl.ds(off, size)],
+                        send_sem=last_send_sem.at[a, g, k],
+                        recv_sem=last_recv_sem.at[a, g, k],
+                        device_id=targets[(a + g) % 3],
+                        device_id_type=MESH,
+                    )
                 )
-            )
         for copy in copies:
             copy.start()
         for copy in copies:
@@ -533,7 +544,9 @@
         logits = logits + jnp.dot(
             value, w_head[h * half : (h + 1) * half, :], preferred_element_type=F32
         )
-    norm_out[...] = jnp.sqrt(square)[: norm_out.shape[0]]
+    requests = norm_out.shape[0]
+    norms = jnp.transpose(jnp.broadcast_to(jnp.sqrt(square), top_mine.shape))
+    norm_out[...] = norms[:1, :requests].reshape(requests)
     best = jnp.max(logits, axis=1, keepdims=True)
     top_mine[...] = jnp.broadcast_to(best, top_mine.shape)
     top_copies = []
@@ -555,7 +568,7 @@
     best = top_mine[...]
     for k in (1, 2, 3):
         best = jnp.maximum(best, top_recv[k])
-    logit_out[...] = best[: logit_out.shape[0], :1]
+    logit_out[...] = jnp.transpose(best)[:1, :requests]
 
     for p in (1, 2, 3):
         meta_copy(p).wait_send()
@@ -601,14 +614,7 @@
     held, _, rank = adapter_down.shape
     columns = head_weight.shape[1]
     requests = lengths.shape[0]
-    meta = jnp.concatenate(
-        [
-            jnp.pad(routes.astype(F32).T, ((0, 2), (0, 0))),
-            jnp.pad(route_gates.astype(F32).T, ((0, 2), (0, 0))),
-        ],
-        axis=0,
-    )
-    low_down = jnp.transpose(adapter_down, (1, 0, 2)).reshape(width, held * rank)
+    low_down = jnp.transpose(adapter_down, (0, 2, 1)).reshape(held * rank, width)
     low_up = adapter_up.reshape(held * rank, width)
     vmem = pl.BlockSpec(memory_space=pltpu.VMEM)
     smem = pl.BlockSpec(memory_space=pltpu.SMEM)
@@ -619,19 +625,19 @@
         body,
         out_shape=(
             jax.ShapeDtypeStruct((rows, width), BF16),
-            jax.ShapeDtypeStruct((requests, 1), F32),
-            jax.ShapeDtypeStruct((requests, 1), F32),
+            jax.ShapeDtypeStruct((requests,), F32),
+            jax.ShapeDtypeStruct((1, requests), F32),
         ),
-        in_specs=[smem] * 3 + [vmem] * 3 + [anywhere] * 9,
+        in_specs=[smem] * 3 + [vmem] * 4 + [anywhere] * 9,
         out_specs=(vmem, vmem, vmem),
         scratch_shapes=[
             pltpu.VMEM((width, inner_width), BF16),
             pltpu.VMEM((width, inner_width), BF16),
             pltpu.VMEM((inner_width, width), BF16),
-            pltpu.VMEM((width, shared_width), BF16),
-            pltpu.VMEM((width, shared_width), BF16),
             pltpu.VMEM((shared_width, width), BF16),
-            pltpu.VMEM((width, held * rank), BF16),
+            pltpu.VMEM((shared_width, width), BF16),
+            pltpu.VMEM((shared_width, width), BF16),
+            pltpu.VMEM((held * rank, width), BF16),
             pltpu.VMEM((held * rank, width), BF16),
             pltpu.VMEM((width, columns), BF16),
             pltpu.VMEM((4, rows, width), BF16),
@@ -673,8 +679,8 @@
             dma((4,)),
             dma((2,)),
             dma((2,)),
-            dma((3, 4)),
-            dma((3, 4)),
+            dma((3, 3, 4)),
+            dma((3, 3, 4)),
             dma((4,)),
             dma((4,)),
         ],
@@ -687,19 +693,20 @@
         request_adapter,
         adapter_slot,
         tokens,
-        norm_gain.reshape(1, width),
-        meta,
+        norm_gain,
+        routes.T,
+        route_gates.T,
         expert_gate,
         expert_up,
         expert_down,
-        shared_gate,
-        shared_up_weight,
+        shared_gate.T,
+        shared_up_weight.T,
         shared_down,
         low_down,
         low_up,
         head_weight,
     )
-    return (sublayer, last_norm.reshape(requests), block_logit)
+    return (sublayer, last_norm, block_logit.T)
 
 
 def solution(mesh):

time: 128 us -> 114 us (0.89)
  local copies, waits for them, and re-layouts: 10.8 us -> 4.17 us
  Pallas kernels: 113 us -> 109 us
  other arithmetic: 3.31 us -> 0 us
    reshape x2 -> x0, local copies, waits for them, and re-layouts: 3.33 us -> none  [the longest x1 2.04 us: local(): jnp.transpose(adapter_down, (1, 0, 2)).reshape(width, held * rank)]
    unnamed x6 -> x3, local copies, waits for them, and re-layouts: 7.43 us -> 4.17 us
    pallas_call x1, Pallas kernels: 113 us -> 109 us  [local(): pl.pallas_call(body, out_shape=(jax.ShapeDtypeStruct((rows, width), BF16)...]
    pallas_call x1 -> x0, other arithmetic: 1.33 us -> none  [local(): pl.pallas_call(body, out_shape=(jax.ShapeDtypeStruct((rows, width), BF16)...]
where the time goes in v2:
time: 114 us
  Pallas kernels  109 us (96%)
  local copies, waits for them, and re-layouts  4.17 us (4%)
    pallas_call x1, Pallas kernels, local(): pl.pallas_call(body, out_shape=(jax.ShapeDtypeStruct((rows, width), BF16)...  109 us
    unnamed x3, local copies, waits for them, and re-layouts  4.17 us

profile of v2, /device:TPU:1, one launch (start us, length us, event | category | flops | bytes accessed | tf_op | source)
XLA Modules:
  0.0 114.3 jit_solution(15166785742077072453)
XLA Ops:
  0.6 109.5 %sublayer.1 = (bf16[128,2048]{1,0:T(8,128)(2,1)}, f32[24]{0:T(128)}, f32[1,24]{1,0:T(1,128)}) custom-call(s32[24]{0:T(128)} %lengths.1, s32[24]{0:T(128)} %request_adapter.1, s32[32]{0:T(128)} %adapter_slot.1, bf16[128,2048]{1,0:T(8,128)(2,1)} %tokens.1, bf16[2048]{0:T(1024)(128)(2,1)} %gain.1, s32[6,128]{1,0:T(8,128)} %bitcast.13, bf16[6,128]{1,0:T(8,128)(2,1)} %bitcast.14, ...), custom_call_target="tpu_custom_call" | custom-call | tf_op jit(solution)/shard_map/sublayer/pallas_call | solution.py:624
  110.1 1.9 %copy.22 = bf16[128,2048]{1,0:T(8,128)(2,1)} copy(bf16[128,2048]{1,0:T(8,128)(2,1)} %get-tuple-element.12) | data formatting | bytes 1048576
  112.0 1.1 copy.23
  113.1 1.2 %copy.24 = f32[24,1]{0,1:T(1,128)} copy(f32[24,1]{0,1:T(1,128)} %bitcast.15) | data formatting | bytes 192

commit v3 on v2

--- a/solution.py
+++ b/solution.py
@@ -397,7 +397,9 @@
 
         lax.fori_loop(0, width // 512, columns, 0)
 
-    def select_step(p, carry):
+    def select_step(i, carry):
+        p = (i + 1) % 4
+
         @pl.when(p > 0)
         def _():
             pltpu.make_async_remote_copy(
@@ -438,33 +440,35 @@
     for load in loads[5:8]:
         load.wait()
 
-    def expert_step(p, carry):
-        expert(p)
-
-        @pl.when(p < 2)
+    def combine_step(p):
+        combine(p, False)
+        part_copy(p, jnp.where(p == 2, 3, jnp.where(p == 3, 2, p))).start()
+
+    def expert_step(i, carry):
+        expert((i + 1) % 4)
+
+        @pl.when(i < 2)
         def _():
-            shared_step(p, 0)
-
-            @pl.when(p == 0)
+            shared_step(i, 0)
+
+            @pl.when(i == 0)
             def _():
                 shared_copy(1).start()
 
-            @pl.when(p == 1)
+            @pl.when(i == 1)
             def _():
                 shared_copy(2).start()
                 shared_copy(3).start()
 
+        @pl.when(i > 1)
+        def _():
+            combine_step(i - 1)
+
         return carry
 
     lax.fori_loop(0, 4, expert_step, 0)
+    combine_step(3)
     combine(0, True)
-
-    def combine_step(p, carry):
-        combine(p, False)
-        part_copy(p, jnp.where(p == 2, 3, jnp.where(p == 3, 2, p))).start()
-        return carry
-
-    lax.fori_loop(1, 4, combine_step, 0)
 
     for p in (1, 2, 3):
         shared_copy(p).wait_recv()

time: 114 us -> 112 us (0.982)
  Pallas kernels: 109 us -> 107 us
    pallas_call x1, Pallas kernels: 109 us -> 107 us  [local(): pl.pallas_call(body, out_shape=(jax.ShapeDtypeStruct((rows, width), BF16)...]
where the time goes in v3:
time: 112 us
  Pallas kernels  107 us (96%)
  local copies, waits for them, and re-layouts  4.17 us (4%)
    pallas_call x1, Pallas kernels, local(): pl.pallas_call(body, out_shape=(jax.ShapeDtypeStruct((rows, width), BF16)...  107 us
    unnamed x3, local copies, waits for them, and re-layouts  4.17 us

profile of v3, /device:TPU:1, one launch (start us, length us, event | category | flops | bytes accessed | tf_op | source)
XLA Modules:
  0.0 111.7 jit_solution(12157687516332962701)
XLA Ops:
  0.6 106.9 %sublayer.1 = (bf16[128,2048]{1,0:T(8,128)(2,1)}, f32[24]{0:T(128)}, f32[1,24]{1,0:T(1,128)}) custom-call(s32[24]{0:T(128)} %lengths.1, s32[24]{0:T(128)} %request_adapter.1, s32[32]{0:T(128)} %adapter_slot.1, bf16[128,2048]{1,0:T(8,128)(2,1)} %tokens.1, bf16[2048]{0:T(1024)(128)(2,1)} %gain.1, s32[6,128]{1,0:T(8,128)} %bitcast.13, bf16[6,128]{1,0:T(8,128)(2,1)} %bitcast.14, ...), custom_call_target="tpu_custom_call" | custom-call | tf_op jit(solution)/shard_map/sublayer/pallas_call | solution.py:628
  107.5 1.9 %copy.22 = bf16[128,2048]{1,0:T(8,128)(2,1)} copy(bf16[128,2048]{1,0:T(8,128)(2,1)} %get-tuple-element.12) | data formatting | bytes 1048576
  109.4 1.1 copy.23
  110.5 1.2 %copy.24 = f32[24,1]{0,1:T(1,128)} copy(f32[24,1]{0,1:T(1,128)} %bitcast.15) | data formatting | bytes 192

commit v4 on v3

--- a/solution.py
+++ b/solution.py
@@ -460,14 +460,15 @@
                 shared_copy(2).start()
                 shared_copy(3).start()
 
-        @pl.when(i > 1)
-        def _():
-            combine_step(i - 1)
-
         return carry
 
     lax.fori_loop(0, 4, expert_step, 0)
-    combine_step(3)
+
+    def combine_all(p, carry):
+        combine_step(p)
+        return carry
+
+    lax.fori_loop(1, 4, combine_all, 0)
     combine(0, True)
 
     for p in (1, 2, 3):

time: 112 us -> 111 us (level)
  no operation moved by 1% of the time
where the time goes in v4:
time: 111 us
  Pallas kernels  106 us (95%)
  local copies, waits for them, and re-layouts  4.17 us (4%)
    pallas_call x1, Pallas kernels, local(): pl.pallas_call(body, out_shape=(jax.ShapeDtypeStruct((rows, width), BF16)...  106 us
    unnamed x3, local copies, waits for them, and re-layouts  4.17 us

profile of v4, /device:TPU:1, one launch (start us, length us, event | category | flops | bytes accessed | tf_op | source)
XLA Modules:
  0.0 110.6 jit_solution(12973815121920734306)
XLA Ops:
  0.6 105.8 %sublayer.1 = (bf16[128,2048]{1,0:T(8,128)(2,1)}, f32[24]{0:T(128)}, f32[1,24]{1,0:T(1,128)}) custom-call(s32[24]{0:T(128)} %lengths.1, s32[24]{0:T(128)} %request_adapter.1, s32[32]{0:T(128)} %adapter_slot.1, bf16[128,2048]{1,0:T(8,128)(2,1)} %tokens.1, bf16[2048]{0:T(1024)(128)(2,1)} %gain.1, s32[6,128]{1,0:T(8,128)} %bitcast.13, bf16[6,128]{1,0:T(8,128)(2,1)} %bitcast.14, ...), custom_call_target="tpu_custom_call" | custom-call | tf_op jit(solution)/shard_map/sublayer/pallas_call | solution.py:629
  106.5 1.9 %copy.22 = bf16[128,2048]{1,0:T(8,128)(2,1)} copy(bf16[128,2048]{1,0:T(8,128)(2,1)} %get-tuple-element.12) | data formatting | bytes 1048576
  108.3 1.1 copy.23
  109.4 1.2 %copy.24 = f32[24,1]{0,1:T(1,128)} copy(f32[24,1]{0,1:T(1,128)} %bitcast.15) | data formatting | bytes 192
